TPU v7x, 512 devices: a whole 4x4x16 slice. The times are simulated.
512 devices in a mesh: dp: 64 (over y_hi, z, core), seq: 8 (over x, y_lo).
Axes of the slice: x: 4, y: 4 (y_hi: 2, y_lo: 2; y = y_hi * 2 + y_lo), z: 16, core: 2. Of those that a mesh axis runs over, the one named last changes fastest.
Arguments:
- queries: bfloat16 [65536, 4096], P(('dp', 'seq')), may hold values from -180 to 180, as said below
- keys: bfloat16 [65536, 512], P(('dp', 'seq')), may hold values from -6 to 6, as said below
- values: bfloat16 [65536, 512], P(('dp', 'seq')), may hold values from -6 to 6
- lengths: int32 [64, 16], P('dp'), may hold values from 1 to 512, 1024 in all within a row
- out_grad: bfloat16 [65536, 4096], P(('dp', 'seq')), may hold values from -6 to 6
Outputs:
- attended: bfloat16 [65536, 4096], P(('dp', 'seq'))
- query_grad: bfloat16 [65536, 4096], P(('dp', 'seq'))
- key_grad: bfloat16 [65536, 512], P(('dp', 'seq'))
- value_grad: bfloat16 [65536, 512], P(('dp', 'seq'))
Inputs may be any that keep to these rules, and one draw needn't show every extreme that they name: `queries`: queries stay within this range. `keys`: keys stay within this range.
All inputs are finite; a program needn't handle non-finite values.
Results may differ from a plain program's by a relative error of at most 0.0095.
Values may be sent and summed in bfloat16 or wider, within the bound.
No kernel may reach another device: no remote copies, remote signals or barrier semaphores. Data moves between devices by JAX's collectives and lax.ppermute only.
A program may use at most 64 MiB of HBM per device.

v0:
```python
import jax
import jax.numpy as jnp
from jax import lax
from jax.sharding import PartitionSpec as P

H = 32
KVH = 4
HD = 128
GROUP = 8


def doc_of(pos, ends):
    return jnp.sum((pos[:, None] >= ends[None, :]).astype(jnp.int32), axis=1)


def shards(queries, keys, values, lengths, out_grad):
    tok_rows = queries.shape[0]
    kv_width = keys.shape[1]
    scale = HD ** (-0.5)
    qh = queries.reshape(tok_rows, KVH, GROUP, HD)
    grad_heads = out_grad.reshape(tok_rows, KVH, GROUP, HD)
    ends = jnp.cumsum(lengths[0])
    seq_pos = lax.axis_index("seq") * tok_rows + jnp.arange(tok_rows, dtype=jnp.int32)
    query_doc = doc_of(seq_pos, ends)
    total_len = tok_rows * lax.axis_size("seq")
    block = min(512, total_len)
    live_blocks = seq_pos[-1] // block + 1

    def visible_of(kstart, count):
        kpos = kstart + jnp.arange(count, dtype=jnp.int32)
        return (doc_of(kpos, ends)[None, :] == query_doc[:, None]) & (
            kpos[None, :] <= seq_pos[:, None]
        )

    def scores_of(key_rows, visible):
        raw = (
            jnp.einsum(
                "tkgd,skd->kgts",
                qh,
                key_rows.reshape(-1, KVH, HD),
                preferred_element_type=jnp.float32,
            )
            * scale
        )
        return jnp.where(visible, raw, -1e30)

    def forward_step(carry, key_rows, value_rows, kstart):
        top, lsum, acc = carry
        visible = visible_of(kstart, key_rows.shape[0])
        scores = scores_of(key_rows, visible)
        top_new = jnp.maximum(top, jnp.max(scores, axis=-1))
        rescale = jnp.exp(top - top_new)
        expo = jnp.where(visible, jnp.exp(scores - top_new[..., None]), 0.0)
        lsum = lsum * rescale + jnp.sum(expo, axis=-1)
        acc = acc * rescale[..., None] + jnp.einsum(
            "kgts,skd->kgtd",
            expo.astype(jnp.bfloat16),
            value_rows.reshape(-1, KVH, HD),
            preferred_element_type=jnp.float32,
        )
        return (top_new, lsum, acc)

    start_carry = (
        jnp.full((KVH, GROUP, tok_rows), -1e30, jnp.float32),
        jnp.zeros((KVH, GROUP, tok_rows), jnp.float32),
        jnp.zeros((KVH, GROUP, tok_rows, HD), jnp.float32),
    )
    key_all, value_all = (
        lax.all_gather(keys, "seq", axis=0, tiled=True),
        lax.all_gather(values, "seq", axis=0, tiled=True),
    )

    def forward_block(index, carry):
        kstart = index * block
        key_rows = lax.dynamic_slice_in_dim(key_all, kstart, block, 0)
        value_rows = lax.dynamic_slice_in_dim(value_all, kstart, block, 0)
        return forward_step(carry, key_rows, value_rows, kstart)

    top, lsum, acc = lax.fori_loop(0, live_blocks, forward_block, start_carry)
    heads_out = acc / lsum[..., None]
    attended = heads_out.transpose(2, 0, 1, 3).reshape(tok_rows, H * HD).astype(jnp.bfloat16)
    rowdot = jnp.sum(
        out_grad.astype(jnp.float32).reshape(tok_rows, KVH, GROUP, HD)
        * attended.astype(jnp.float32).reshape(tok_rows, KVH, GROUP, HD),
        axis=-1,
    ).transpose(1, 2, 0)

    def backward_block(index, carry):
        query_acc, partial_value = carry
        kstart = index * block
        key_rows = lax.dynamic_slice_in_dim(key_all, kstart, block, 0)
        value_rows = lax.dynamic_slice_in_dim(value_all, kstart, block, 0)
        visible = visible_of(kstart, block)
        scores = scores_of(key_rows, visible)
        probs = jnp.where(visible, jnp.exp(scores - top[..., None]) / lsum[..., None], 0.0)
        value_heads = value_rows.reshape(block, KVH, HD)
        key_heads = key_rows.reshape(block, KVH, HD)
        dprobs = jnp.einsum(
            "tkgd,skd->kgts", grad_heads, value_heads, preferred_element_type=jnp.float32
        )
        dscores = (probs * (dprobs - rowdot[..., None])).astype(jnp.bfloat16)
        query_acc = query_acc + jnp.einsum(
            "kgts,skd->kgtd", dscores, key_heads, preferred_element_type=jnp.float32
        )
        key_part = (
            jnp.einsum("kgts,tkgd->skd", dscores, qh, preferred_element_type=jnp.float32) * scale
        )
        value_part = jnp.einsum(
            "kgts,tkgd->skd",
            probs.astype(jnp.bfloat16),
            grad_heads,
            preferred_element_type=jnp.float32,
        )
        stacked = jnp.concatenate(
            [key_part.reshape(block, kv_width), value_part.reshape(block, kv_width)], axis=1
        )
        partial_value = lax.dynamic_update_slice(
            partial_value, stacked.astype(jnp.bfloat16), (kstart, 0)
        )
        return (query_acc, partial_value)

    back_carry = (
        jnp.zeros((KVH, GROUP, tok_rows, HD), jnp.float32),
        jnp.zeros((total_len, 2 * kv_width), jnp.bfloat16),
    )
    query_acc, partial_value = lax.fori_loop(0, live_blocks, backward_block, back_carry)
    summed = lax.psum_scatter(partial_value, "seq", scatter_dimension=0, tiled=True).astype(
        jnp.float32
    )
    query_grad = (
        (query_acc * scale).transpose(2, 0, 1, 3).reshape(tok_rows, H * HD).astype(jnp.bfloat16)
    )
    key_grad = summed[:, :kv_width].astype(jnp.bfloat16)
    value_grad = summed[:, kv_width:].astype(jnp.bfloat16)
    return (attended, query_grad, key_grad, value_grad)


def solution(mesh):
    in_specs = (
        P(("dp", "seq"), None),
        P(("dp", "seq"), None),
        P(("dp", "seq"), None),
        P("dp", None),
        P(("dp", "seq"), None),
    )
    out_specs = (
        P(("dp", "seq"), None),
        P(("dp", "seq"), None),
        P(("dp", "seq"), None),
        P(("dp", "seq"), None),
    )
    return jax.shard_map(shards, mesh=mesh, in_specs=in_specs, out_specs=out_specs, check_vma=False)
```

profile of v0, /device:TPU:42, one launch (start us, length us, event | category | flops | bytes accessed | tf_op | source)
XLA Modules:
  0.0 249.3 jit_solution(3896361902892705112)
XLA Ops:
  7.2 0.0 all-gather.3.cloned.1.call-start
  7.2 1.7 copy.56
  8.9 0.0 all-gather.3.cloned.1.call-update
  8.9 0.0 all-gather.5.cloned.1.call-start
  8.9 1.7 copy.58
  10.6 0.0 all-gather.5.cloned.1.call-update
  10.6 0.0 reduce-scatter.2.cloned.1.call-start
  10.7 0.6 slice.11
  13.9 0.7 copy.55
  14.7 0.1 reduce
  14.8 1.6 copy.62
  16.4 2.3 copy.57
  18.7 1.6 copy.59
  20.3 0.1 convert_reduce_fusion.2
  20.4 42.1 %all-gather.3.cloned.1.call-done = bf16[1024,512]{0,1:T(8,128)(2,1)} async-done(((bf16[128,512]{0,1:T(8,128)(2,1)}), bf16[1024,512]{0,1:T(8,128)(2,1)}) %all-gather.3.cloned.1.call-update) | async-done | bytes 1048592 | tf_op jit(solution)/shard_map/all_gather | solution.py:69
  62.5 53.0 %all-gather.5.cloned.1.call-done = bf16[1024,512]{0,1:T(8,128)(2,1)} async-done(((bf16[128,512]{0,1:T(8,128)(2,1)}), bf16[1024,512]{0,1:T(8,128)(2,1)}) %all-gather.5.cloned.1.call-update) | async-done | bytes 1048592 | tf_op jit(solution)/shard_map/all_gather | solution.py:70
  115.5 1.6 broadcast.53.clone
  117.1 10.0 %while.28 = (s32[]{:T(128)}, f32[4,8,128]{2,1,0:T(8,128)S(1)}, f32[4,8,128]{2,1,0:T(8,128)S(1)}, f32[4,8,128,128]{3,2,1,0:T(8,128)}, s32[]{:T(128)}, /*index=5*/...) while((s32[]{:T(128)}, f32[4,8,128]{2,1,0:T(8,128)S(1)}, ...), condition=%wide.region_6.7_spmd.clone, body=%wide.region_2.6_spmd.clone.sunk | while | flops 1102282880 | bytes 50868028 | solution.py:79
  117.1 0.1 convert_reduce_fusion.5
  117.2 0.2 compare_and_fusion.4
  117.4 1.3 constant_dynamic-slice_fusion.6
  118.7 1.5 fusion.69
  120.1 0.0 copy-start
  120.2 2.1 fusion.70
  122.3 0.0 copy-done
  122.3 3.4 %multiply_add_fusion.5 = f32[4,8,128,128]{3,2,1,0:T(8,128)S(1)} fusion(f32[4,8,128,128]{3,2,1,0:T(8,128)S(1)} %copy-done, bf16[512,4,128,1]{0,2,3,1:T(8,128)(2,1)S(1)} %bitcast.153, f32[4,512,128,8]{2,1,3,0:T(8,128)S(1)} %get-tuple-element.446, f32[4,8,128]{2,1,0:T(8,128)S(1)} %max.5, pred[128,512]{0,1:T(8,128)(4,1)S(1)} %compare_and_fusion.4, ...), kind=kOutput, calls=%fused_computation.9.clone.1 | convolution fusion | flops 548405248 | bytes 13205504 | tf_op jit(solution)/shard_map/while/body/kgts,skd->kgtd/dot_general | solution.py:55
  125.7 0.0 copy-start.1
  125.7 1.3 copy-done.1
  127.1 1.9 copy.60
  129.0 1.5 multiply_reduce_fusion
  130.5 1.6 broadcast.53
  132.1 1.6 broadcast_in_dim.53.clone
  133.7 17.2 %while.29 = (s32[]{:T(128)}, f32[4,8,128,128]{3,2,1,0:T(8,128)}, bf16[1024,1024]{1,0:T(8,128)(2,1)}, s32[]{:T(128)}, s32[16]{0:T(128)S(1)}, /*index=5*/s32[128]{...) while((s32[]{:T(128)}, f32[4,8,128,128]{3,2,1,0:T(8,128)}, ...), condition=%wide.region_10.11_spmd.clone, body=%wide.region_8.10_spmd.clone.sunk | while | flops 2706857984 | bytes 57339684 | solution.py:126
  133.7 0.1 convert_reduce_fusion.6
  133.8 0.2 compare_and_fusion.5
  134.0 1.3 constant_dynamic-slice_fusion.7
  135.3 3.8 %fusion.81 = f32[4,8,128,512]{2,3,1,0:T(8,128)S(1)} fusion(f32[4,8,128]{2,1,0:T(8,128)S(1)} %get-tuple-element.556, f32[4,8,128]{2,1,0:T(8,128)S(1)} %get-tuple-element.555, pred[128,512]{0,1:T(8,128)(4,1)S(1)} %compare_and_fusion.5, bf16[512,4,128,1]{0,2,3,1:T(8,128)(2,1)S(1)} %bitcast.149, bf16[128,4,8,128]{0,3,2,1:T(8,128)(2,1)} %get-tuple-element.554), kind=kOutput, calls=%fused_computation.28.clone.1 | convolution fusion | flops 547356672 | bytes 10059776 | tf_op jit(solution)/shard_map/while/body/tkgd,skd->kgts/dot_general | solution.py:37
  139.1 1.5 fusion.83
  140.6 1.4 fusion.82
  142.0 2.7 %fusion.84 = bf16[4,512,128]{1,2,0:T(8,128)(2,1)S(1)} fusion(bf16[4,8,128,512]{2,3,1,0:T(8,128)(2,1)S(1)} %fusion.82, bf16[128,4,8,128]{0,3,2,1:T(8,128)(2,1)} %get-tuple-element.554), kind=kOutput, calls=%fused_computation.36.clone.1 | convolution fusion | flops 537395200 | bytes 5767168 | tf_op jit(solution)/shard_map/while/body/kgts,tkgd->skd/dot_general | solution.py:106
  144.7 4.5 %convolution_add_fusion.2 = f32[4,8,128,128]{3,2,1,0:T(8,128)} fusion(f32[4,8,128,128]{3,2,1,0:T(8,128)} %get-tuple-element.530, bf16[4,8,128,512]{2,3,1,0:T(8,128)(2,1)S(1)} %fusion.82, bf16[512,4,128,1]{0,2,3,1:T(8,128)(2,1)S(1)} %bitcast.150), kind=kOutput, calls=%fused_computation.31.clone.1 | convolution fusion | flops 537395200 | bytes 8912896 | tf_op jit(solution)/shard_map/while/body/kgts,skd->kgtd/dot_general | solution.py:102
  149.2 0.1 pad_maximum_fusion.2
  149.3 0.5 copy.95
  149.9 1.1 constant_dynamic-update-slice_fusion.2
  150.9 0.0 reduce-scatter.2.cloned.1.call-update
  150.9 2.3 copy.78
  153.2 1.9 fusion.31
  155.1 0.7 copy.63
  155.8 1.4 copy.93
  157.2 83.9 %reduce-scatter.2.cloned.1.call-done = bf16[128,1024]{1,0:T(8,128)(2,1)} async-done(((bf16[1024,1024]{1,0:T(8,128)(2,1)}), bf16[128,1024]{1,0:T(8,128)(2,1)}) %reduce-scatter.2.cloned.1.call-update) | async-done | bytes 262160 | tf_op jit(solution)/shard_map/reduce_scatter | solution.py:127
  241.1 1.7 fusion.32
  (11 shorter events, 0.1 us)
Async XLA Ops:
  7.2 55.3 %all-gather.3.cloned.1.call-start = ((), (), s32[]{:S(2)}) async-start(), calls=%async_computation.1 | async-start | bytes 1179648 | tf_op jit(solution)/shard_map/all_gather | solution.py:69
  8.9 106.6 %all-gather.5.cloned.1.call-start = ((), (), s32[]{:S(2)}) async-start(), calls=%async_computation.2 | async-start | bytes 1179648 | tf_op jit(solution)/shard_map/all_gather | solution.py:70
  10.6 230.4 %reduce-scatter.2.cloned.1.call-start = ((), (), s32[]{:S(2)}) async-start(), calls=%async_computation.3 | async-start | bytes 2359296 | tf_op jit(solution)/shard_map/reduce_scatter | solution.py:127
  120.1 2.2 copy-start
  125.7 1.4 copy-start.1
Sparse Core Ops, SparseCore 0:
  10.6 51.9 all-gather.2
  65.1 50.3 all-gather.4
  151.1 89.9 reduce-scatter.1
where the time goes:
time: 250 us; the launch traced here: 249 us
  waiting for transfers between devices  179 us (72%)
  local copies, waits for them, and re-layouts  28.3 us (11%)
  matrix products  18.8 us (8%)
  between operations  16.4 us (7%)
  other arithmetic  6.46 us (3%)
    reduce_scatter x1, waiting for transfers between devices, shards(): lax.psum_scatter(partial_value, 'seq', scatter_dimension=0, tiled=True)  83.9 us
    all_gather x1, waiting for transfers between devices, shards(): lax.all_gather(values, 'seq', axis=0, tiled=True)  53 us
    all_gather x1, waiting for transfers between devices, shards(): lax.all_gather(keys, 'seq', axis=0, tiled=True)  42.1 us
    unnamed x6, local copies, waits for them, and re-layouts  10.2 us
    dot_general x2, matrix products, scores_of(): jnp.einsum('tkgd,skd->kgts', qh, key_rows.reshape(-1, KVH, HD), preferred...  5.27 us
  transfers between devices with their start and end apart: 3, of which 3 were waited for; matrix products, arithmetic and copies ran while one was open for 6% of the time, Pallas kernels for 0%

commit v1 on v0

--- a/solution.py
+++ b/solution.py
@@ -7,6 +7,11 @@
 KVH = 4
 HD = 128
 GROUP = 8
+
+
+def all_by_exchange(shard, axis, dim):
+    sent = jnp.stack([shard] * lax.axis_size(axis))
+    return jnp.concatenate(lax.all_to_all(sent, axis, 0, 0), axis=dim)
 
 
 def doc_of(pos, ends):
@@ -67,7 +72,7 @@
     )
     key_all, value_all = (
         lax.all_gather(keys, "seq", axis=0, tiled=True),
-        lax.all_gather(values, "seq", axis=0, tiled=True),
+        all_by_exchange(values, "seq", 0),
     )
 
     def forward_block(index, carry):

time: 250 us -> 198 us (0.79)
  the two profiles are of different devices: /device:TPU:42 before, /device:TPU:10 now
where the time goes in v1:
time: 198 us; the launch traced here: 197 us
  waiting for transfers between devices  114 us (58%)
  local copies, waits for them, and re-layouts  31.5 us (16%)
  matrix products  18.8 us (9%)
  between operations  16.7 us (8%)
  starting transfers between devices  9.28 us (5%)
  other arithmetic  6.46 us (3%)
    reduce_scatter x1, waiting for transfers between devices, shards(): lax.psum_scatter(partial_value, 'seq', scatter_dimension=0, tiled=True)  85.1 us
    all_gather x1, waiting for transfers between devices, shards(): lax.all_gather(keys, 'seq', axis=0, tiled=True)  26.8 us
    unnamed x9, local copies, waits for them, and re-layouts  11 us
    all_to_all x1, starting transfers between devices, all_by_exchange(): return jnp.concatenate(lax.all_to_all(sent, axis, 0, 0), axis=dim)  9.24 us
    dot_general x2, matrix products, scores_of(): jnp.einsum('tkgd,skd->kgts', qh, key_rows.reshape(-1, KVH, HD), preferred...  5.27 us
    dot_general x1, matrix products, backward_block(): jnp.einsum('kgts,skd->kgtd', dscores, key_heads, preferred_element_type=j...  4.52 us
  transfers between devices with their start and end apart: 3, of which 3 were waited for; matrix products, arithmetic and copies ran while one was open for 9% of the time, Pallas kernels for 0%

profile of v1, /device:TPU:10, one launch (start us, length us, event | category | flops | bytes accessed | tf_op | source)
XLA Modules:
  0.0 197.1 jit_solution(447239484237575102)
XLA Ops:
  7.2 0.0 copy-start.2
  7.2 0.0 all-gather.2.cloned.1.call-start
  7.2 1.7 copy.101
  9.0 0.0 all-gather.2.cloned.1.call-update
  9.0 1.0 copy.103
  10.0 1.1 stack.2
  11.1 9.2 %all-to-all-start = ((bf16[8,128,512]{1,2,0:T(8,128)(2,1)}), bf16[8,128,512]{1,2,0:T(8,128)(2,1)S(1)}, u32[]{:S(2)}, u32[]{:S(2)}) async-start(bf16[8,128,512]{1,2,0:T(8,128)(2,1)} %stack.2), calls=%async_computation | async-start | bytes 2097152 | tf_op jit(solution)/shard_map/all_to_all | solution.py:14
  20.4 0.0 reduce-scatter.2.cloned.1.call-start
  20.4 0.6 slice.11
  23.6 0.7 copy.100
  24.3 0.1 reduce
  24.5 0.0 copy-done.2
  24.5 0.7 copy.109
  25.1 2.3 %copy.102 = bf16[128,4096]{0,1:T(8,128)(2,1)} copy(bf16[128,4096]{1,0:T(8,128)(2,1)} %param.9) | data formatting | bytes 2097152 | tf_op args[0]
  27.4 1.6 copy.105
  29.0 0.1 convert_reduce_fusion.2
  29.1 2.3 %all-to-all-done = bf16[8,128,512]{1,2,0:T(8,128)(2,1)S(1)} async-done(((bf16[8,128,512]{1,2,0:T(8,128)(2,1)}), bf16[8,128,512]{1,2,0:T(8,128)(2,1)S(1)}, u32[]{:S(2)}, u32[]{:S(2)}) %all-to-all-start) | async-done | bytes 1048608 | tf_op jit(solution)/shard_map/all_to_all | solution.py:14
  31.4 1.3 copy.104
  32.7 2.3 %copy.106 = bf16[1024,512]{0,1:T(8,128)(2,1)} copy(bf16[1024,512]{1,0:T(8,128)(2,1)} %bitcast.156) | data formatting | bytes 2097152
  35.0 26.8 %all-gather.2.cloned.1.call-done = bf16[1024,512]{0,1:T(8,128)(2,1)} async-done(((bf16[128,512]{0,1:T(8,128)(2,1)}), bf16[1024,512]{0,1:T(8,128)(2,1)}) %all-gather.2.cloned.1.call-update) | async-done | bytes 1048592 | tf_op jit(solution)/shard_map/all_gather | solution.py:74
  61.8 1.6 broadcast.55.clone
  63.4 10.0 %while.28 = (s32[]{:T(128)}, f32[4,8,128]{2,1,0:T(8,128)S(1)}, f32[4,8,128]{2,1,0:T(8,128)S(1)}, f32[4,8,128,128]{3,2,1,0:T(8,128)}, s32[]{:T(128)}, /*index=5*/...) while((s32[]{:T(128)}, f32[4,8,128]{2,1,0:T(8,128)S(1)}, ...), condition=%wide.region_6.7_spmd.clone, body=%wide.region_2.6_spmd.clone.sunk | while | flops 1102282880 | bytes 50868028 | solution.py:84
  63.4 0.1 convert_reduce_fusion.5
  63.5 0.2 compare_and_fusion.4
  63.7 1.3 constant_dynamic-slice_fusion.6
  65.0 1.5 fusion.69
  66.4 0.0 copy-start
  66.5 2.1 %fusion.70 = f32[4,8,128]{2,1,0:T(8,128)S(1)} fusion(f32[4,512,128,8]{2,1,3,0:T(8,128)S(1)} %get-tuple-element.496, f32[4,8,128]{2,1,0:T(8,128)S(1)} %max.5, pred[128,512]{0,1:T(8,128)(4,1)S(1)} %compare_and_fusion.4), kind=kLoop, calls=%fused_computation.6.clone.1 | loop fusion | flops 10481664 | bytes 8486912 | tf_op jit(solution)/shard_map/while/body/reduce_sum | solution.py:59
  68.6 0.0 copy-done
  68.6 3.4 %multiply_add_fusion.5 = f32[4,8,128,128]{3,2,1,0:T(8,128)S(1)} fusion(f32[4,8,128,128]{3,2,1,0:T(8,128)S(1)} %copy-done, bf16[512,4,128,1]{0,2,3,1:T(8,128)(2,1)S(1)} %bitcast.154, f32[4,512,128,8]{2,1,3,0:T(8,128)S(1)} %get-tuple-element.496, f32[4,8,128]{2,1,0:T(8,128)S(1)} %max.5, pred[128,512]{0,1:T(8,128)(4,1)S(1)} %compare_and_fusion.4, ...), kind=kOutput, calls=%fused_computation.9.clone.1 | convolution fusion | flops 548405248 | bytes 13205504 | tf_op jit(solution)/shard_map/while/body/kgts,skd->kgtd/dot_general | solution.py:60
  72.0 0.0 copy-start.1
  72.0 1.3 copy-done.1
  73.4 1.9 copy.107
  75.3 1.5 multiply_reduce_fusion
  76.8 1.6 broadcast.55
  78.4 1.6 broadcast_in_dim.53.clone
  80.0 17.2 %while.29 = (s32[]{:T(128)}, f32[4,8,128,128]{3,2,1,0:T(8,128)}, bf16[1024,1024]{1,0:T(8,128)(2,1)}, s32[]{:T(128)}, s32[16]{0:T(128)S(1)}, /*index=5*/s32[128]{...) while((s32[]{:T(128)}, f32[4,8,128,128]{3,2,1,0:T(8,128)}, ...), condition=%wide.region_10.11_spmd.clone, body=%wide.region_8.10_spmd.clone.sunk | while | flops 2706857984 | bytes 57339684 | solution.py:131
  80.0 0.1 convert_reduce_fusion.6
  80.1 0.2 compare_and_fusion.5
  80.3 1.3 constant_dynamic-slice_fusion.7
  81.6 3.8 %fusion.81 = f32[4,8,128,512]{2,3,1,0:T(8,128)S(1)} fusion(f32[4,8,128]{2,1,0:T(8,128)S(1)} %get-tuple-element.606, f32[4,8,128]{2,1,0:T(8,128)S(1)} %get-tuple-element.605, pred[128,512]{0,1:T(8,128)(4,1)S(1)} %compare_and_fusion.5, bf16[512,4,128,1]{0,2,3,1:T(8,128)(2,1)S(1)} %bitcast.150, bf16[128,4,8,128]{0,3,2,1:T(8,128)(2,1)} %get-tuple-element.604), kind=kOutput, calls=%fused_computation.28.clone.1 | convolution fusion | flops 547356672 | bytes 10059776 | tf_op jit(solution)/shard_map/while/body/tkgd,skd->kgts/dot_general | solution.py:42
  85.4 1.5 fusion.83
  86.9 1.4 fusion.82
  88.3 2.7 %fusion.84 = bf16[4,512,128]{1,2,0:T(8,128)(2,1)S(1)} fusion(bf16[4,8,128,512]{2,3,1,0:T(8,128)(2,1)S(1)} %fusion.82, bf16[128,4,8,128]{0,3,2,1:T(8,128)(2,1)} %get-tuple-element.604), kind=kOutput, calls=%fused_computation.36.clone.1 | convolution fusion | flops 537395200 | bytes 5767168 | tf_op jit(solution)/shard_map/while/body/kgts,tkgd->skd/dot_general | solution.py:111
  91.0 4.5 %convolution_add_fusion.2 = f32[4,8,128,128]{3,2,1,0:T(8,128)} fusion(f32[4,8,128,128]{3,2,1,0:T(8,128)} %get-tuple-element.580, bf16[4,8,128,512]{2,3,1,0:T(8,128)(2,1)S(1)} %fusion.82, bf16[512,4,128,1]{0,2,3,1:T(8,128)(2,1)S(1)} %bitcast.151), kind=kOutput, calls=%fused_computation.31.clone.1 | convolution fusion | flops 537395200 | bytes 8912896 | tf_op jit(solution)/shard_map/while/body/kgts,skd->kgtd/dot_general | solution.py:107
  95.5 0.1 pad_maximum_fusion.2
  95.6 0.5 copy.143
  96.2 1.1 constant_dynamic-update-slice_fusion.2
  97.2 0.0 reduce-scatter.2.cloned.1.call-update
  97.2 2.3 %copy.126 = bf16[128,4096]{1,0:T(8,128)(2,1)} copy(bf16[128,4096]{0,1:T(8,128)(2,1)} %bitcast.158) | data formatting | bytes 2097152 | tf_op jit(solution)/shard_map/convert_element_type | solution.py:86
  99.5 1.9 fusion.31
  101.4 0.7 copy.111
  102.1 1.4 copy.141
  103.5 85.1 %reduce-scatter.2.cloned.1.call-done = bf16[128,1024]{1,0:T(8,128)(2,1)} async-done(((bf16[1024,1024]{1,0:T(8,128)(2,1)}), bf16[128,1024]{1,0:T(8,128)(2,1)}) %reduce-scatter.2.cloned.1.call-update) | async-done | bytes 262160 | tf_op jit(solution)/shard_map/reduce_scatter | solution.py:132
  188.6 1.7 fusion.32
  (11 shorter events, 0.1 us)
Async XLA Ops:
  7.2 17.3 %copy-start.2 = (bf16[128,4096]{1,0:T(8,128)(2,1)S(1)}, bf16[128,4096]{1,0:T(8,128)(2,1)}, u32[]{:S(2)}) copy-start(bf16[128,4096]{1,0:T(8,128)(2,1)} %param.13) | copy-start | bytes 3145732
  7.2 54.6 %all-gather.2.cloned.1.call-start = ((), (), s32[]{:S(2)}) async-start(), calls=%async_computation.2 | async-start | bytes 1179648 | tf_op jit(solution)/shard_map/all_gather | solution.py:74
  11.1 20.2 %all-to-all-start = ((bf16[8,128,512]{1,2,0:T(8,128)(2,1)}), bf16[8,128,512]{1,2,0:T(8,128)(2,1)S(1)}, u32[]{:S(2)}, u32[]{:S(2)}) async-start(bf16[8,128,512]{1,2,0:T(8,128)(2,1)} %stack.2), calls=%async_computation | async-start | bytes 2097152 | tf_op jit(solution)/shard_map/all_to_all | solution.py:14
  20.4 168.2 %reduce-scatter.2.cloned.1.call-start = ((), (), s32[]{:S(2)}) async-start(), calls=%async_computation.3 | async-start | bytes 2359296 | tf_op jit(solution)/shard_map/reduce_scatter | solution.py:132
  66.4 2.2 %copy-start = (f32[4,8,128,128]{3,2,1,0:T(8,128)S(1)}, f32[4,8,128,128]{3,2,1,0:T(8,128)}, u32[]{:S(2)}) copy-start(f32[4,8,128,128]{3,2,1,0:T(8,128)} %get-tuple-element.534) | copy-start | bytes 6291460 | tf_op jit(solution)/shard_map/while
  72.0 1.4 copy-start.1
Sparse Core Ops, SparseCore 0:
  10.6 51.1 all-gather.1
  97.4 91.1 reduce-scatter.1
